TPU v7x, 32 devices: a whole 2x2x4 slice. The times are simulated.
32 devices in a mesh: fsdp: 2 (over x), ctx: 4 (over y, core), tp: 4 (over z).
Axes of the slice: x: 2, y: 2, z: 4, core: 2. Of those that a mesh axis runs over, the one named last changes fastest.
Arguments:
- tokens: bfloat16 [2, 1152, 1024], P('fsdp', 'ctx'), may hold values from -6 to 6
- segment_ids: int32 [2, 1152], P('fsdp'), may hold values from 0 to 2, never falling along the last dimension, each value on 1 to 576 neighbouring positions
- first_gain: bfloat16 [1024], P(('fsdp', 'ctx')), may hold values from 0.5 to 1.5
- first_shift: bfloat16 [1024], P(('fsdp', 'ctx')), may hold values from -3 to 3
- input_weight: bfloat16 [3, 1024, 1024], P(None, ('fsdp', 'ctx'), 'tp'), may hold values from -0.1875 to 0.1875
- input_bias: bfloat16 [2, 1024], P(None, 'tp'), may hold values from -3 to 3
- output_weight: bfloat16 [1024, 1024], P('tp', ('fsdp', 'ctx')), may hold values from -0.75 to 0.75
- output_bias: bfloat16 [1024], P(('fsdp', 'ctx')), may hold values from -3 to 3
- second_gain: bfloat16 [1024], P(('fsdp', 'ctx')), may hold values from 0.5 to 1.5
- second_shift: bfloat16 [1024], P(('fsdp', 'ctx')), may hold values from -3 to 3
- up_weight: bfloat16 [1024, 4096], P(('fsdp', 'ctx'), 'tp'), may hold values from -0.1875 to 0.1875
- up_bias: bfloat16 [4096], P('tp'), may hold values from -3 to 3
- down_weight: bfloat16 [4096, 1024], P('tp', ('fsdp', 'ctx')), may hold values from -0.125 to 0.125
- down_bias: bfloat16 [1024], P(('fsdp', 'ctx')), may hold values from -3 to 3
- cotangent: bfloat16 [2, 1152, 1024], P('fsdp', 'ctx'), may hold values from -6 to 6
Outputs:
- result: bfloat16 [2, 1152, 1024], P('fsdp', 'ctx')
- tokens_grad: float32 [2, 1152, 1024], P('fsdp', 'ctx')
- first_gain_grad: float32 [1024], P(('fsdp', 'ctx'))
- first_shift_grad: float32 [1024], P(('fsdp', 'ctx'))
- input_weight_grad: float32 [3, 1024, 1024], P(None, ('fsdp', 'ctx'), 'tp')
- input_bias_grad: float32 [2, 1024], P(None, 'tp')
- output_weight_grad: float32 [1024, 1024], P('tp', ('fsdp', 'ctx'))
- output_bias_grad: float32 [1024], P(('fsdp', 'ctx'))
- second_gain_grad: float32 [1024], P(('fsdp', 'ctx'))
- second_shift_grad: float32 [1024], P(('fsdp', 'ctx'))
- up_weight_grad: float32 [1024, 4096], P(('fsdp', 'ctx'), 'tp')
- up_bias_grad: float32 [4096], P('tp')
- down_weight_grad: float32 [4096, 1024], P('tp', ('fsdp', 'ctx'))
- down_bias_grad: float32 [1024], P(('fsdp', 'ctx'))
Inputs may be any that keep to these rules, and one draw needn't show every extreme that they name: `segment_ids`: along each sequence the ids never fall; each id covers 1 to 576 consecutive positions.
All inputs are finite; a program needn't handle non-finite values.
Results may differ from a plain program's by a relative error of at most 0.017.
Values may be sent and summed in bfloat16 or wider, within the bound.
No kernel may reach another device: no remote copies, remote signals or barrier semaphores. Data moves between devices by JAX's collectives and lax.ppermute only.
A program may use at most 128 MiB of HBM per device.

v0:
```python
from functools import partial
import math

import jax
import jax.numpy as jnp
from jax import lax
from jax.experimental import pallas as pl
from jax.sharding import PartitionSpec as P


HEAD_DIM = 64
MAX_SEGMENT = 576
EPSILON = 1e-05
FC = ("fsdp", "ctx")
BF = jnp.bfloat16
F32 = jnp.float32


def swap(x, axis, offset):
    size = lax.axis_size(axis)
    return lax.ppermute(x, axis, [(i, i ^ offset) for i in range(size)])


def order(size):
    return [2 * i for i in range(size // 2)] + [2 * i + 1 for i in range(size // 2)]


def place_of(offset, size):
    return (offset & 1) * (size // 2) + (offset >> 1)


def device_index():
    return lax.axis_index("fsdp") * lax.axis_size("ctx") + lax.axis_index("ctx")


def group_size():
    return lax.axis_size("fsdp") * lax.axis_size("ctx")


def to_relative(x):
    size, me = group_size(), device_index()
    width = x.shape[1] // size
    return jnp.concatenate(
        [lax.dynamic_slice_in_dim(x, (me ^ o) * width, width, 1) for o in order(size)], axis=1
    )


def to_absolute(x):
    size, me = group_size(), device_index()
    width = x.shape[1] // size
    return jnp.concatenate(
        [
            lax.dynamic_slice_in_dim(x, place_of(me ^ j, size) * width, width, 1)
            for j in range(size)
        ],
        axis=1,
    )


def join_kernel(*refs):
    out_ref = refs[-1]
    width = refs[0].shape[1]
    for i, ref in enumerate(refs[:-1]):
        out_ref[:, i * width : (i + 1) * width] = ref[...]


def join(pieces):
    rows, width = pieces[0].shape
    tile = max(d for d in range(16, min(rows, 1024) + 1, 16) if rows % d == 0)
    total = width * len(pieces)
    return pl.pallas_call(
        join_kernel,
        grid=(rows // tile,),
        in_specs=[pl.BlockSpec((tile, width), lambda i: (i, 0))] * len(pieces),
        out_specs=pl.BlockSpec((tile, total), lambda i: (i, 0)),
        out_shape=jax.ShapeDtypeStruct((rows, total), pieces[0].dtype),
        cost_estimate=pl.CostEstimate(
            flops=0, bytes_accessed=4 * rows * total, transcendentals=0
        ),
        name="join",
    )(*pieces)


def gather_columns(w):
    size = group_size()
    if size > 8:
        picked = jnp.take(
            lax.all_gather(w, FC), device_index() ^ jnp.array(order(size)), axis=0
        )
        full = jnp.moveaxis(picked, 0, 1).reshape(w.shape[0], -1)
        return jnp.split(full, 2, axis=1)
    pieces = [w] + [swap(w, FC, o) for o in order(size)[1 : size // 2]]
    even = join(pieces)
    return even, swap(even, FC, 1)


def scatter_sum(even, odd, axis):
    size = group_size()
    half = size // 2
    if size > 8:
        pieces = jnp.stack(jnp.split(even, half, axis) + jnp.split(odd, half, axis)).astype(BF)
        wanted = place_of(device_index() ^ jnp.arange(size), size)
        parts = lax.all_to_all(jnp.take(pieces, wanted, axis=0), FC, 0, 0, tiled=True)
        return jnp.sum(parts.astype(F32), axis=0)
    summed = even.astype(F32) + swap(odd.astype(BF), FC, 1).astype(F32)
    pieces = jnp.split(summed, half, axis)
    total = pieces[0]
    for o, piece in zip(order(size)[1:half], pieces[1:]):
        total = total + swap(piece.astype(BF), FC, o).astype(F32)
    return total


def sum_all(x, axis, size):
    step = 1
    while step < size:
        x = x + swap(x, axis, step)
        step *= 2
    return x


def sum_direct(x, axis, size):
    pieces = [x] + [swap(x, axis, s) for s in range(1, size)]
    while len(pieces) > 1:
        pieces = [a + b for a, b in zip(pieces[::2], pieces[1::2])]
    return pieces[0]


def row_block(x, index, rows):
    return lax.dynamic_slice_in_dim(x, index * rows, rows, 0)


def tp_scatter_rows(halves):
    tp, t = lax.axis_size("tp"), lax.axis_index("tp")
    rows = halves[0].shape[0] // tp
    total = jnp.concatenate([row_block(h, t, rows) for h in halves], axis=1)
    for s in range(1, tp):
        block = [row_block(h, t ^ s, rows).astype(BF) for h in halves]
        block = jnp.concatenate(block, axis=1) if len(block) > 1 else block[0]
        total = total + swap(block, "tp", s).astype(F32)
    return total


def put_rows(pieces):
    tp, t = lax.axis_size("tp"), lax.axis_index("tp")
    rows = pieces[0].shape[0]
    out = jnp.zeros((rows * tp, pieces[0].shape[1]), pieces[0].dtype)
    for s, piece in enumerate(pieces):
        out = lax.dynamic_update_slice_in_dim(out, piece, (t ^ s) * rows, 0)
    return out


def tp_gather_rows(x, dtype):
    tp = lax.axis_size("tp")
    pieces = [x] + [swap(x, "tp", s) for s in range(1, tp)]
    return put_rows([piece.astype(dtype) for piece in pieces])


def normalise(x):
    center = x - jnp.mean(x, axis=-1, keepdims=True)
    inverse = lax.rsqrt(jnp.mean(center * center, axis=-1, keepdims=True) + EPSILON)
    return center * inverse, inverse


def normalise_back(grad, gain, xhat, inverse):
    gx = grad * gain
    mean_gx = jnp.mean(gx, axis=-1, keepdims=True)
    mean_gxx = jnp.mean(gx * xhat, axis=-1, keepdims=True)
    return (gx - mean_gx - xhat * mean_gxx) * inverse


def nt(a, b):
    return lax.dot_general(a, b, (((1,), (1,)), ((), ())), preferred_element_type=F32)


def mm(a, b):
    return jnp.dot(a, b, preferred_element_type=F32)


def tn(a, b):
    return lax.dot_general(a, b, (((0,), (0,)), ((), ())), preferred_element_type=F32)


def attend_kernel(blocks, *refs):
    q_ref, bias_ref = refs[0], refs[1]
    k_refs, v_refs = refs[2 : 2 + blocks], refs[2 + blocks : 2 + 2 * blocks]
    out_ref, total_ref = refs[2 + 2 * blocks :]
    rows = q_ref.shape[0]
    for h in range(q_ref.shape[1] // HEAD_DIM):
        cols = slice(h * HEAD_DIM, (h + 1) * HEAD_DIM)
        q = q_ref[:, cols]
        scores = [
            nt(k_refs[b][:, cols], q) + bias_ref[b * rows : (b + 1) * rows, :]
            for b in range(blocks)
        ]
        highest = scores[0].max(axis=0, keepdims=True)
        for s in scores[1:]:
            highest = jnp.maximum(highest, s.max(axis=0, keepdims=True))
        weights = [jnp.exp(s - highest) for s in scores]
        summed = sum(w.sum(axis=0, keepdims=True) for w in weights)
        scale = 1.0 / summed
        mixed = sum(
            tn(v_refs[b][:, cols], (weights[b] * scale).astype(BF)) for b in range(blocks)
        )
        out_ref[:, cols] = mixed.T.astype(BF)
        total_ref[0, h : h + 1, :] = highest + jnp.log(summed)


def attend_back_kernel(blocks, *refs):
    q_ref, grad_ref, bias_ref, total_ref = refs[:4]
    kv_refs, outs = refs[4 : 4 + blocks], refs[4 + blocks :]
    gq_ref, gkv_refs = outs[0], outs[1:]
    rows, width = q_ref.shape
    for h in range(q_ref.shape[1] // HEAD_DIM):
        cols = slice(h * HEAD_DIM, (h + 1) * HEAD_DIM)
        q, grad = q_ref[:, cols], grad_ref[:, cols]
        values = slice(width + h * HEAD_DIM, width + (h + 1) * HEAD_DIM)
        total = total_ref[h // 2, h % 2 : h % 2 + 1, :]
        probs, grads = [], []
        for b in range(blocks):
            s = nt(kv_refs[b][:, cols], q) + bias_ref[b * rows : (b + 1) * rows, :]
            probs.append(jnp.exp(s - total))
            grads.append(nt(kv_refs[b][:, values], grad))
        inner = sum((p * g).sum(axis=0, keepdims=True) for p, g in zip(probs, grads))
        gq = None
        for b in range(blocks):
            gs = (probs[b] * (grads[b] - inner)).astype(BF)
            gk = jnp.dot(gs, q, preferred_element_type=F32)
            gv = jnp.dot(probs[b].astype(BF), grad, preferred_element_type=F32)
            low, high = h * HEAD_DIM, (h + 1) * HEAD_DIM
            gkv_refs[b][:, low:high] = gk.astype(gkv_refs[b].dtype)
            gkv_refs[b][:, width + low : width + high] = gv.astype(gkv_refs[b].dtype)
            part = tn(kv_refs[b][:, cols], gs)
            gq = part if gq is None else gq + part
        gq_ref[:, cols] = (gq.T * (1.0 / math.sqrt(HEAD_DIM))).astype(gq_ref.dtype)


def attention_specs(rows, width, blocks):
    pair = 2 * HEAD_DIM
    steps = width // pair
    tile = pl.BlockSpec((rows, pair), lambda j: (0, j))
    value_tile = pl.BlockSpec((rows, pair), lambda j: (0, steps + j))
    bias = pl.BlockSpec((blocks * rows, rows), lambda j: (0, 0))
    total = pl.BlockSpec((1, 2, rows), lambda j: (j, 0, 0))
    return steps, tile, value_tile, bias, total


def attend(q, kv, bias):
    rows, width = q.shape
    blocks = len(kv)
    steps, tile, value_tile, bias_spec, total = attention_specs(rows, width, blocks)
    return pl.pallas_call(
        partial(attend_kernel, blocks),
        grid=(steps,),
        in_specs=[tile, bias_spec] + [tile] * blocks + [value_tile] * blocks,
        out_specs=[tile, total],
        out_shape=[
            jax.ShapeDtypeStruct((rows, width), BF),
            jax.ShapeDtypeStruct((steps, 2, rows), F32),
        ],
        cost_estimate=pl.CostEstimate(
            flops=4 * blocks * rows * rows * width,
            bytes_accessed=4 * blocks * rows * (rows + width),
            transcendentals=blocks * rows * rows * width // HEAD_DIM,
        ),
        name="attend",
    )(q, bias, *kv, *kv)


def attend_back(q, kv, bias, totals, grad):
    rows, width = q.shape
    blocks = len(kv)
    kinds = [F32] + [BF] * (blocks - 1)
    return pl.pallas_call(
        partial(attend_back_kernel, blocks),
        out_shape=[jax.ShapeDtypeStruct((rows, width), BF)]
        + [jax.ShapeDtypeStruct((rows, 2 * width), k) for k in kinds],
        cost_estimate=pl.CostEstimate(
            flops=10 * blocks * rows * rows * width,
            bytes_accessed=4 * blocks * rows * (rows + width),
            transcendentals=blocks * rows * rows * width // HEAD_DIM,
        ),
        name="attend_back",
    )(q, grad, bias, totals, *kv)


def local(
    tokens,
    segment_ids,
    first_gain,
    first_shift,
    input_weight,
    input_bias,
    output_weight,
    output_bias,
    second_gain,
    second_shift,
    up_weight,
    up_bias,
    down_weight,
    down_bias,
    cotangent,
):
    sequences, rows, features = tokens.shape
    ctx, tp = lax.axis_size("ctx"), lax.axis_size("tp")
    c, t = lax.axis_index("ctx"), lax.axis_index("tp")
    size = group_size()
    half = features // 2
    chunk = rows // tp
    width = input_weight.shape[2]
    earlier = min(ctx - 1, -(-(MAX_SEGMENT - 1) // rows))
    blocks = earlier + 1

    vectors = jnp.stack(
        [first_gain, first_shift, output_bias, second_gain, second_shift, down_bias]
    )
    first_shard = jnp.concatenate(
        [
            jnp.swapaxes(input_weight, 1, 2).reshape(3 * width, -1),
            jnp.pad(vectors, ((0, 26), (0, 0))),
        ],
        axis=0,
    )
    first_full = join(list(gather_columns(first_shard)))
    in_full = first_full[: 3 * width]
    vectors_full = first_full[3 * width :].astype(F32)
    gain_one, shift_one, out_shift, gain_two, shift_two, down_shift = [
        vectors_full[i : i + 1] for i in range(6)
    ]
    out_rows = jnp.concatenate(
        [output_weight] + [swap(output_weight, "tp", s) for s in range(1, tp)], axis=0
    )
    ff_shard = jnp.concatenate([up_weight.T, down_weight], axis=0)

    resid = to_relative(tokens.reshape(rows, features)).astype(F32)
    cot_low = to_relative(cotangent.reshape(rows, features))
    xhat_one, inverse_one = normalise(resid)
    normed_low = (xhat_one * gain_one + shift_one).astype(BF)

    ids = segment_ids.reshape(-1)
    query_seg = lax.dynamic_slice_in_dim(ids, c * rows, rows, 0)
    padded = jnp.concatenate([jnp.full((earlier * rows,), -1, ids.dtype), ids])
    biases = []
    for b in range(blocks):
        key_seg = lax.dynamic_slice_in_dim(padded, (c + earlier - b) * rows, rows, 0)
        allowed = key_seg[:, None] == query_seg[None, :]
        if b == 0:
            place = jnp.arange(rows)
            allowed = allowed & (place[:, None] <= place[None, :])
        biases.append(jnp.where(allowed, 0.0, -1e30).astype(F32))
    bias = jnp.concatenate(biases, axis=0)

    in_bias = jnp.concatenate([input_bias[0], jnp.zeros_like(input_bias[0]), input_bias[1]])
    projected = (nt(normed_low, in_full) + in_bias.astype(F32)).astype(BF)
    queries = projected[:, :width] * jnp.asarray(1.0 / math.sqrt(HEAD_DIM), BF)
    kv = [projected[:, width:]]
    for b in range(1, blocks):
        kv.append(lax.ppermute(kv[0], "ctx", [(i, i + b) for i in range(ctx - b)]))
    out_full = join(list(gather_columns(out_rows)))
    ff_halves = gather_columns(ff_shard)
    hidden_width = up_weight.shape[1]
    up_even, up_odd = [w[:hidden_width] for w in ff_halves]
    down_even, down_odd = [w[hidden_width:] for w in ff_halves]

    mixed, totals = attend(queries, kv, bias)
    mixed_all = jnp.concatenate([mixed] + [swap(mixed, "tp", s) for s in range(1, tp)], axis=1)
    middle = resid + out_shift + jnp.dot(mixed_all, out_full, preferred_element_type=F32)
    xhat_two, inverse_two = normalise(middle)
    normed_two = (xhat_two * gain_two + shift_two).astype(BF)
    hidden = nt(normed_two[:, :half], up_even) + nt(normed_two[:, half:], up_odd)
    hidden = hidden + up_bias.astype(F32)
    gelu_tanh = partial(jax.nn.gelu, approximate=True)
    active, gelu_pullback = jax.vjp(gelu_tanh, hidden)
    active = active.astype(BF)
    grad_active = nt(cot_low[:, :half], down_even) + nt(cot_low[:, half:], down_odd)
    grad_hidden = gelu_pullback(grad_active)[0].astype(BF)
    grad_norm_two = tp_scatter_rows([mm(grad_hidden, up_even), mm(grad_hidden, up_odd)])
    up_grad = scatter_sum(
        tn(normed_two[:, :half], grad_hidden), tn(normed_two[:, half:], grad_hidden), 0
    )
    down_grad = scatter_sum(tn(active, cot_low[:, :half]), tn(active, cot_low[:, half:]), 1)
    grad_up_bias = jnp.sum(grad_hidden.astype(F32), axis=0)

    middle_rows = row_block(middle, t, chunk)
    xhat_rows, inverse_rows = row_block(xhat_two, t, chunk), row_block(inverse_two, t, chunk)
    cot_rows = row_block(cot_low, t, chunk).astype(F32)
    grad_middle = cot_rows + normalise_back(grad_norm_two, gain_two, xhat_rows, inverse_rows)
    grad_attn = grad_middle.astype(BF)
    grad_mixed = nt(grad_attn, out_full).astype(BF)
    grad_pieces = jnp.split(grad_mixed, tp, axis=1)
    mixed_rows = row_block(mixed_all, t, chunk)
    grad_heads = put_rows([grad_pieces[0]] + [swap(grad_pieces[s], "tp", s) for s in range(1, tp)])

    mlp_halves = [mm(active, down_even), mm(active, down_odd)]
    result_rows = middle_rows + tp_scatter_rows(mlp_halves) + down_shift
    result = tp_gather_rows(to_absolute(result_rows.astype(BF)), BF)

    grads = attend_back(queries, kv, bias, totals, grad_heads)
    grad_queries = grads[0]
    grad_kv = grads[1]
    for b in range(1, blocks):
        back = [(i + b, i) for i in range(ctx - b)]
        arrived = lax.ppermute(grads[1 + b], "ctx", back)
        grad_kv = grad_kv + arrived.astype(F32)
    grad_joined = jnp.concatenate([grad_queries, grad_kv.astype(BF)], axis=1)
    out_grad = scatter_sum(
        tn(mixed_rows, grad_attn[:, :half]), tn(mixed_rows, grad_attn[:, half:]), 1
    )
    out_blocks = jnp.split(out_grad, tp, axis=0)
    out_weight_grad = out_blocks[0]
    for s in range(1, tp):
        out_weight_grad = out_weight_grad + swap(out_blocks[s].astype(BF), "tp", s).astype(F32)

    grad_norm_one = tp_scatter_rows([mm(grad_joined, in_full)])
    in_grad = scatter_sum(
        tn(normed_low[:, :half], grad_joined), tn(normed_low[:, half:], grad_joined), 0
    )
    in_weight_grad = jnp.stack([in_grad[:, i * width : (i + 1) * width] for i in range(3)])
    grad_in_bias = jnp.sum(grad_joined.astype(F32), axis=0)
    grad_in_bias = jnp.concatenate([grad_in_bias[:width], grad_in_bias[2 * width :]])
    bias_sums = sum_all(jnp.concatenate([grad_in_bias, grad_up_bias])[None, :], FC, size)[0]

    xhat_one_rows = row_block(xhat_one, t, chunk)
    inverse_one_rows = row_block(inverse_one, t, chunk)
    tokens_grad_rows = grad_middle + normalise_back(
        grad_norm_one, gain_one, xhat_one_rows, inverse_one_rows
    )
    tokens_grad = tp_gather_rows(to_absolute(tokens_grad_rows.astype(BF)), F32)

    sums = jnp.stack(
        [
            jnp.sum(grad_norm_one * xhat_one_rows, axis=0),
            jnp.sum(grad_norm_one, axis=0),
            jnp.sum(grad_attn.astype(F32), axis=0),
            jnp.sum(grad_norm_two * xhat_rows, axis=0),
            jnp.sum(grad_norm_two, axis=0),
            jnp.sum(cot_rows, axis=0),
        ]
    )
    sums = sum_direct(sums, "tp", tp)
    vector_grads = scatter_sum(sums[:, :half], sums[:, half:], 1)
    return (
        result.reshape(sequences, rows, features),
        tokens_grad.reshape(sequences, rows, features),
        vector_grads[0],
        vector_grads[1],
        in_weight_grad,
        bias_sums[: 2 * width].reshape(2, width),
        out_weight_grad,
        vector_grads[2],
        vector_grads[3],
        vector_grads[4],
        up_grad,
        bias_sums[2 * width :],
        down_grad,
        vector_grads[5],
    )


def solution(mesh):
    in_specs = (
        P("fsdp", "ctx", None),
        P("fsdp", None),
        P(("fsdp", "ctx")),
        P(("fsdp", "ctx")),
        P(None, ("fsdp", "ctx"), "tp"),
        P(None, "tp"),
        P("tp", ("fsdp", "ctx")),
        P(("fsdp", "ctx")),
        P(("fsdp", "ctx")),
        P(("fsdp", "ctx")),
        P(("fsdp", "ctx"), "tp"),
        P("tp"),
        P("tp", ("fsdp", "ctx")),
        P(("fsdp", "ctx")),
        P("fsdp", "ctx", None),
    )
    out_specs = (
        P("fsdp", "ctx", None),
        P("fsdp", "ctx", None),
        P(("fsdp", "ctx")),
        P(("fsdp", "ctx")),
        P(None, ("fsdp", "ctx"), "tp"),
        P(None, "tp"),
        P("tp", ("fsdp", "ctx")),
        P(("fsdp", "ctx")),
        P(("fsdp", "ctx")),
        P(("fsdp", "ctx")),
        P(("fsdp", "ctx"), "tp"),
        P("tp"),
        P("tp", ("fsdp", "ctx")),
        P(("fsdp", "ctx")),
    )
    return jax.shard_map(
        local,
        mesh=mesh,
        in_specs=in_specs,
        out_specs=out_specs,
        check_vma=False,
    )
```

profile of v0, /device:TPU:0, one launch (start us, length us, event | category | flops | bytes accessed | tf_op | source)
XLA Modules:
  0.0 315.3 jit_solution(5934195008093835319)
XLA Ops:
  2.6 3.1 collective-permute-start
  28.8 9.9 %collective-permute-done.12.refs_1_ = bf16[1024,128]{1,0:T(8,128)(2,1)} collective-permute-done((bf16[1024,128]{1,0:T(8,128)(2,1)S(1)}, bf16[1024,128]{1,0:T(8,128)(2,1)}, u32[]{:S(2)}, u32[]{:S(2)}) %collective-permute-start.12) | collective-permute-done | bytes 262176 | tf_op jit(solution)/shard_map/ppermute | solution.py:21
  40.6 12.8 %collective-permute-done.13.refs_2_ = bf16[1024,128]{1,0:T(8,128)(2,1)S(1)} collective-permute-done((bf16[1024,128]{1,0:T(8,128)(2,1)S(1)}, bf16[1024,128]{1,0:T(8,128)(2,1)S(1)}, u32[]{:S(2)}, u32[]{:S(2)}) %collective-permute-start.13) | collective-permute-done | bytes 262176 | tf_op jit(solution)/shard_map/ppermute | solution.py:21
  55.1 5.7 %collective-permute-done.14.refs_3_ = bf16[1024,128]{1,0:T(8,128)(2,1)} collective-permute-done((bf16[1024,128]{1,0:T(8,128)(2,1)S(1)}, bf16[1024,128]{1,0:T(8,128)(2,1)}, u32[]{:S(2)}, u32[]{:S(2)}) %collective-permute-start.14) | collective-permute-done | bytes 262176 | tf_op jit(solution)/shard_map/ppermute | solution.py:21
  80.6 5.1 %collective-permute-done.5.refs_4_.refs_7_.refs_6_ = bf16[288,512]{1,0:T(8,128)(2,1)S(1)} collective-permute-done((bf16[288,512]{1,0:T(8,128)(2,1)S(1)}, bf16[288,512]{1,0:T(8,128)(2,1)S(1)}, u32[]{:S(2)}, u32[]{:S(2)}) %collective-permute-start.5) | collective-permute-done | bytes 294944 | tf_op jit(solution)/shard_map/ppermute | solution.py:357
  86.4 6.0 %attend.1 = (bf16[288,256]{1,0:T(8,128)(2,1)}, f32[2,2,288]{2,1,0:T(2,128)}) custom-call(bf16[288,256]{1,0:T(8,128)(2,1)} %slice_multiply_fusion.refs_0_, f32[864,288]{1,0:T(8,128)} %pad_maximum_fusion.refs_1_.refs_2_, bf16[288,512]{1,0:T(8,128)(2,1)} %copy-done.1, bf16[288,512]{1,0:T(8,128)(2,1)} %copy-done.2, bf16[288,512]{1,0:T(8,128)(2,1)} %copy-done.3, ...), custom_call_target="tpu_custom_call" | custom-call | flops 254803968 | bytes 1880064 | tf_op jit(solution)/shard_map/attend/pallas_call | solution.py:251
  95.9 6.4 %collective-permute-start.7 = (bf16[288,256]{1,0:T(8,128)(2,1)}, bf16[288,256]{1,0:T(8,128)(2,1)}, u32[]{:S(2)}, u32[]{:S(2)}) collective-permute-start(bf16[288,256]{1,0:T(8,128)(2,1)} %get-tuple-element.20), channel_id=1, source_target_pairs={{0,2},{1,3},{2,0},{3,1},{4,6},{5,7},{6,4},{7,5},{8,10},{9,11},{10,... | collective-permute-start | bytes 442376 | tf_op jit(solution)/shard_map/ppermute | solution.py:21
  103.3 3.0 join.8
  106.4 6.7 %collective-permute-done.7 = bf16[288,256]{1,0:T(8,128)(2,1)} collective-permute-done((bf16[288,256]{1,0:T(8,128)(2,1)}, bf16[288,256]{1,0:T(8,128)(2,1)}, u32[]{:S(2)}, u32[]{:S(2)}) %collective-permute-start.7) | collective-permute-done | bytes 147488 | tf_op jit(solution)/shard_map/ppermute | solution.py:21
  141.3 7.2 %collective-permute-start.26 = (bf16[72,1024]{1,0:T(8,128)(2,1)S(1)}, bf16[72,1024]{1,0:T(8,128)(2,1)S(1)}, u32[]{:S(2)}, u32[]{:S(2)}) collective-permute-start(bf16[72,1024]{1,0:T(8,128)(2,1)S(1)} %pad_maximum_fusion.9), channel_id=1, source_target_pairs={{0,1},{1,0},{2,3},{3,2},{4,5},{5,4},{6,7},{7,6},{8,9},{9,8},{10,11... | collective-permute-start | bytes 442376 | tf_op jit(solution)/shard_map/ppermute | solution.py:21
  148.5 8.1 %collective-permute-done.21 = bf16[72,1024]{1,0:T(8,128)(2,1)S(1)} collective-permute-done((bf16[72,1024]{1,0:T(8,128)(2,1)S(1)}, bf16[72,1024]{1,0:T(8,128)(2,1)S(1)}, u32[]{:S(2)}, u32[]{:S(2)}) %collective-permute-start.21) | collective-permute-done | bytes 147488 | tf_op jit(solution)/shard_map/ppermute | solution.py:21
  161.5 3.2 %collective-permute-start.24 = (bf16[72,1024]{1,0:T(8,128)(2,1)}, bf16[72,1024]{1,0:T(8,128)(2,1)}, u32[]{:S(2)}, u32[]{:S(2)}) collective-permute-start(bf16[72,1024]{1,0:T(8,128)(2,1)} %constant_dynamic-update-slice_fusion.16), channel_id=1, source_target_pairs={{0,2},{1,3},{2,0},{3,1},{4,6},{5,7},{6,4},{7,5},{8,10},{9,11},{10,... | collective-permute-start | bytes 442376 | tf_op jit(solution)/shard_map/ppermute | solution.py:21
  172.2 4.2 %collective-permute-done.29 = bf16[72,256]{1,0:T(8,128)(2,1)S(1)} collective-permute-done((bf16[72,256]{1,0:T(8,128)(2,1)S(1)}, bf16[72,256]{1,0:T(8,128)(2,1)S(1)}, u32[]{:S(2)}, u32[]{:S(2)}) %collective-permute-start.29) | collective-permute-done | bytes 36896 | tf_op jit(solution)/shard_map/ppermute | solution.py:21
  176.8 4.5 %collective-permute-done.30 = bf16[72,256]{1,0:T(8,128)(2,1)S(1)} collective-permute-done((bf16[72,256]{1,0:T(8,128)(2,1)S(1)}, bf16[72,256]{1,0:T(8,128)(2,1)S(1)}, u32[]{:S(2)}, u32[]{:S(2)}) %collective-permute-start.30) | collective-permute-done | bytes 36896 | tf_op jit(solution)/shard_map/ppermute | solution.py:21
  183.5 3.5 %collective-permute-done.31 = bf16[72,256]{1,0:T(8,128)(2,1)S(1)} collective-permute-done((bf16[72,256]{1,0:T(8,128)(2,1)S(1)}, bf16[72,256]{1,0:T(8,128)(2,1)S(1)}, u32[]{:S(2)}, u32[]{:S(2)}) %collective-permute-start.31) | collective-permute-done | bytes 36896 | tf_op jit(solution)/shard_map/ppermute | solution.py:21
  187.7 7.3 %attend_back.1 = (bf16[288,256]{1,0:T(8,128)(2,1)}, f32[288,512]{1,0:T(8,128)}, bf16[288,512]{1,0:T(8,128)(2,1)}, bf16[288,512]{1,0:T(8,128)(2,1)}) custom-call(bf16[288,256]{1,0:T(8,128)(2,1)} %slice_multiply_fusion.refs_0_, bf16[288,256]{1,0:T(8,128)(2,1)} %copy-done.16, f32[864,288]{1,0:T(8,128)} %pad_maximum_fusion.refs_1_.refs_2_, ...), custom_call_target="tpu_custom_call" | custom-call | flops 637009920 | bytes 1880064 | tf_op jit(solution)/shard_map/attend_back/pallas_call | solution.py:273
  204.6 3.0 collective-permute-start.51
  218.8 5.1 %collective-permute-done.35 = bf16[72,1024]{1,0:T(8,128)(2,1)} collective-permute-done((bf16[72,1024]{1,0:T(8,128)(2,1)}, bf16[72,1024]{1,0:T(8,128)(2,1)}, u32[]{:S(2)}, u32[]{:S(2)}) %collective-permute-start.35) | collective-permute-done | bytes 147488 | tf_op jit(solution)/shard_map/ppermute | solution.py:21
  243.5 4.6 %collective-permute-done.37 = bf16[72,1024]{1,0:T(8,128)(2,1)S(1)} collective-permute-done((bf16[72,1024]{1,0:T(8,128)(2,1)S(1)}, bf16[72,1024]{1,0:T(8,128)(2,1)S(1)}, u32[]{:S(2)}, u32[]{:S(2)}) %collective-permute-start.37) | collective-permute-done | bytes 147488 | tf_op jit(solution)/shard_map/ppermute | solution.py:21
  249.5 7.6 %collective-permute-done.38 = bf16[72,1024]{1,0:T(8,128)(2,1)S(1)} collective-permute-done((bf16[72,1024]{1,0:T(8,128)(2,1)S(1)}, bf16[72,1024]{1,0:T(8,128)(2,1)S(1)}, u32[]{:S(2)}, u32[]{:S(2)}) %collective-permute-start.38) | collective-permute-done | bytes 147488 | tf_op jit(solution)/shard_map/ppermute | solution.py:21
  259.0 5.5 %collective-permute-done.39 = bf16[72,1024]{1,0:T(8,128)(2,1)S(1)} collective-permute-done((bf16[72,1024]{1,0:T(8,128)(2,1)S(1)}, bf16[72,1024]{1,0:T(8,128)(2,1)S(1)}, u32[]{:S(2)}, u32[]{:S(2)}) %collective-permute-start.39) | collective-permute-done | bytes 147488 | tf_op jit(solution)/shard_map/ppermute | solution.py:21
  278.6 3.1 collective-permute-done.63
  288.8 4.2 %collective-permute-done.67 = bf16[1024,128]{1,0:T(8,128)(2,1)S(1)} collective-permute-done((bf16[1024,128]{1,0:T(8,128)(2,1)S(1)}, bf16[1024,128]{1,0:T(8,128)(2,1)S(1)}, u32[]{:S(2)}, u32[]{:S(2)}) %collective-permute-start.67) | collective-permute-done | bytes 262176 | tf_op jit(solution)/shard_map/ppermute | solution.py:21
  300.1 4.2 %collective-permute-done.56 = bf16[1024,128]{1,0:T(8,128)(2,1)S(1)} collective-permute-done((bf16[1024,128]{1,0:T(8,128)(2,1)S(1)}, bf16[1024,128]{1,0:T(8,128)(2,1)S(1)}, u32[]{:S(2)}, u32[]{:S(2)}) %collective-permute-start.56) | collective-permute-done | bytes 262176 | tf_op jit(solution)/shard_map/ppermute | solution.py:21
  (386 shorter events, 179.3 us)
Async XLA Ops:
  2.6 21.9 %collective-permute-start = (bf16[800,128]{1,0:T(8,128)(2,1)S(1)}, bf16[800,128]{1,0:T(8,128)(2,1)}, u32[]{:S(2)}, u32[]{:S(2)}) collective-permute-start(bf16[800,128]{1,0:T(8,128)(2,1)S(1)} %fusion.62.refs_0_), channel_id=1, source_target_pairs={{0,8},{4,12},{8,0},{12,4},{16,24},{20,28},{24,16},{28,20},{1,9},{5... | collective-permute-start | bytes 614408 | tf_op jit(solution)/shard_map/ppermute | solution.py:21
  5.7 20.4 %collective-permute-start.1 = (bf16[800,128]{1,0:T(8,128)(2,1)S(1)}, bf16[800,128]{1,0:T(8,128)(2,1)}, u32[]{:S(2)}, u32[]{:S(2)}) collective-permute-start(bf16[800,128]{1,0:T(8,128)(2,1)S(1)} %fusion.62.refs_0_), channel_id=1, source_target_pairs={{0,16},{4,20},{8,24},{12,28},{16,0},{20,4},{24,8},{28,12},{1,17},{... | collective-permute-start | bytes 614408 | tf_op jit(solution)/shard_map/ppermute | solution.py:21
  7.2 19.4 %collective-permute-start.2 = (bf16[800,128]{1,0:T(8,128)(2,1)S(1)}, bf16[800,128]{1,0:T(8,128)(2,1)}, u32[]{:S(2)}, u32[]{:S(2)}) collective-permute-start(bf16[800,128]{1,0:T(8,128)(2,1)S(1)} %fusion.62.refs_0_), channel_id=1, source_target_pairs={{0,24},{4,28},{8,16},{12,20},{16,8},{20,12},{24,0},{28,4},{1,25},{... | collective-permute-start | bytes 614408 | tf_op jit(solution)/shard_map/ppermute | solution.py:21
  17.1 46.1 %collective-permute-start.16 = (bf16[2048,128]{1,0:T(8,128)(2,1)S(1)}, bf16[2048,128]{1,0:T(8,128)(2,1)S(1)}, u32[]{:S(2)}, u32[]{:S(2)}) collective-permute-start(bf16[2048,128]{1,0:T(8,128)(2,1)S(1)} %pad_maximum_fusion.1.refs_0_), channel_id=1, source_target_pairs={{0,8},{4,12},{8,0},{12,4},{16,24},{20,28},{24,16},{28,20},{1,9},{5... | collective-permute-start | bytes 1572872 | tf_op jit(solution)/shard_map/ppermute | solution.py:21
  24.5 38.6 %collective-permute-start.17 = (bf16[2048,128]{1,0:T(8,128)(2,1)S(1)}, bf16[2048,128]{1,0:T(8,128)(2,1)}, u32[]{:S(2)}, u32[]{:S(2)}) collective-permute-start(bf16[2048,128]{1,0:T(8,128)(2,1)S(1)} %pad_maximum_fusion.1.refs_0_), channel_id=1, source_target_pairs={{0,16},{4,20},{8,24},{12,28},{16,0},{20,4},{24,8},{28,12},{1,17},{... | collective-permute-start | bytes 1572872 | tf_op jit(solution)/shard_map/ppermute | solution.py:21
  26.0 37.1 %collective-permute-start.18 = (bf16[2048,128]{1,0:T(8,128)(2,1)S(1)}, bf16[2048,128]{1,0:T(8,128)(2,1)}, u32[]{:S(2)}, u32[]{:S(2)}) collective-permute-start(bf16[2048,128]{1,0:T(8,128)(2,1)S(1)} %pad_maximum_fusion.1.refs_0_), channel_id=1, source_target_pairs={{0,24},{4,28},{8,16},{12,20},{16,8},{20,12},{24,0},{28,4},{1,25},{... | collective-permute-start | bytes 1572872 | tf_op jit(solution)/shard_map/ppermute | solution.py:21
  28.8 38.3 %collective-permute-start.3 = (bf16[800,512]{1,0:T(8,128)(2,1)}, bf16[800,512]{1,0:T(8,128)(2,1)S(1)}, u32[]{:S(2)}, u32[]{:S(2)}) collective-permute-start(bf16[800,512]{1,0:T(8,128)(2,1)} %join.5.refs_0_), channel_id=1, source_target_pairs={{0,4},{4,0},{8,12},{12,8},{16,20},{20,16},{24,28},{28,24},{1,5},{5... | collective-permute-start | bytes 2457608 | tf_op jit(solution)/shard_map/ppermute | solution.py:21
  63.1 40.2 %collective-permute-start.15 = (bf16[1024,512]{1,0:T(8,128)(2,1)}, bf16[1024,512]{1,0:T(8,128)(2,1)}, u32[]{:S(2)}, u32[]{:S(2)}) collective-permute-start(bf16[1024,512]{1,0:T(8,128)(2,1)} %join.7.refs_0_), channel_id=1, source_target_pairs={{0,4},{4,0},{8,12},{12,8},{16,20},{20,16},{24,28},{28,24},{1,5},{5... | collective-permute-start | bytes 3145736 | tf_op jit(solution)/shard_map/ppermute | solution.py:21
  66.6 51.1 %collective-permute-start.19 = (bf16[2048,512]{1,0:T(8,128)(2,1)}, bf16[2048,512]{1,0:T(8,128)(2,1)}, u32[]{:S(2)}, u32[]{:S(2)}) collective-permute-start(bf16[2048,512]{1,0:T(8,128)(2,1)} %join.9), channel_id=1, source_target_pairs={{0,4},{4,0},{8,12},{12,8},{16,20},{20,16},{24,28},{28,24},{1,5},{5... | collective-permute-start | bytes 6291464 | tf_op jit(solution)/shard_map/ppermute | solution.py:21
  136.0 20.6 %collective-permute-start.21 = (bf16[72,1024]{1,0:T(8,128)(2,1)S(1)}, bf16[72,1024]{1,0:T(8,128)(2,1)S(1)}, u32[]{:S(2)}, u32[]{:S(2)}) collective-permute-start(bf16[72,1024]{1,0:T(8,128)(2,1)S(1)} %pad_maximum_fusion.7), channel_id=1, source_target_pairs={{0,2},{1,3},{2,0},{3,1},{4,6},{5,7},{6,4},{7,5},{8,10},{9,11},{10,... | collective-permute-start | bytes 442376 | tf_op jit(solution)/shard_map/ppermute | solution.py:21
  137.3 19.3 %collective-permute-start.20 = (bf16[72,1024]{1,0:T(8,128)(2,1)S(1)}, bf16[72,1024]{1,0:T(8,128)(2,1)S(1)}, u32[]{:S(2)}, u32[]{:S(2)}) collective-permute-start(bf16[72,1024]{1,0:T(8,128)(2,1)S(1)} %pad_maximum_fusion.6), channel_id=1, source_target_pairs={{0,1},{1,0},{2,3},{3,2},{4,5},{5,4},{6,7},{7,6},{8,9},{9,8},{10,11... | collective-permute-start | bytes 442376 | tf_op jit(solution)/shard_map/ppermute | solution.py:21
  137.7 23.8 %collective-permute-start.28 = (bf16[72,1024]{1,0:T(8,128)(2,1)S(1)}, bf16[72,1024]{1,0:T(8,128)(2,1)S(1)}, u32[]{:S(2)}, u32[]{:S(2)}) collective-permute-start(bf16[72,1024]{1,0:T(8,128)(2,1)S(1)} %pad_maximum_fusion.11), channel_id=1, source_target_pairs={{0,3},{1,2},{2,1},{3,0},{4,7},{5,6},{6,5},{7,4},{8,11},{9,10},{10,... | collective-permute-start | bytes 442376 | tf_op jit(solution)/shard_map/ppermute | solution.py:21
  140.6 24.1 %collective-permute-start.27 = (bf16[72,1024]{1,0:T(8,128)(2,1)S(1)}, bf16[72,1024]{1,0:T(8,128)(2,1)S(1)}, u32[]{:S(2)}, u32[]{:S(2)}) collective-permute-start(bf16[72,1024]{1,0:T(8,128)(2,1)S(1)} %pad_maximum_fusion.10), channel_id=1, source_target_pairs={{0,2},{1,3},{2,0},{3,1},{4,6},{5,7},{6,4},{7,5},{8,10},{9,11},{10,... | collective-permute-start | bytes 442376 | tf_op jit(solution)/shard_map/ppermute | solution.py:21
  141.3 24.6 %collective-permute-start.26 = (bf16[72,1024]{1,0:T(8,128)(2,1)S(1)}, bf16[72,1024]{1,0:T(8,128)(2,1)S(1)}, u32[]{:S(2)}, u32[]{:S(2)}) collective-permute-start(bf16[72,1024]{1,0:T(8,128)(2,1)S(1)} %pad_maximum_fusion.9), channel_id=1, source_target_pairs={{0,1},{1,0},{2,3},{3,2},{4,5},{5,4},{6,7},{7,6},{8,9},{9,8},{10,11... | collective-permute-start | bytes 442376 | tf_op jit(solution)/shard_map/ppermute | solution.py:21
  156.5 108.0 %collective-permute-start.61 = (bf16[512,1024]{1,0:T(8,128)(2,1)}, bf16[512,1024]{1,0:T(8,128)(2,1)}, u32[]{:S(2)}, u32[]{:S(2)}) collective-permute-start(bf16[512,1024]{1,0:T(8,128)(2,1)} %convolution_convert_fusion.1), channel_id=1, source_target_pairs={{0,4},{4,0},{8,12},{12,8},{16,20},{20,16},{24,28},{28,24},{1,5},{5... | collective-permute-start | bytes 3145736 | tf_op jit(solution)/shard_map/ppermute | solution.py:21
  161.5 34.9 %collective-permute-start.23 = (bf16[72,1024]{1,0:T(8,128)(2,1)}, bf16[72,1024]{1,0:T(8,128)(2,1)S(1)}, u32[]{:S(2)}, u32[]{:S(2)}) collective-permute-start(bf16[72,1024]{1,0:T(8,128)(2,1)} %constant_dynamic-update-slice_fusion.16), channel_id=1, source_target_pairs={{0,1},{1,0},{2,3},{3,2},{4,5},{5,4},{6,7},{7,6},{8,9},{9,8},{10,11... | collective-permute-start | bytes 442376 | tf_op jit(solution)/shard_map/ppermute | solution.py:21
  161.5 38.6 %collective-permute-start.24 = (bf16[72,1024]{1,0:T(8,128)(2,1)}, bf16[72,1024]{1,0:T(8,128)(2,1)}, u32[]{:S(2)}, u32[]{:S(2)}) collective-permute-start(bf16[72,1024]{1,0:T(8,128)(2,1)} %constant_dynamic-update-slice_fusion.16), channel_id=1, source_target_pairs={{0,2},{1,3},{2,0},{3,1},{4,6},{5,7},{6,4},{7,5},{8,10},{9,11},{10,... | collective-permute-start | bytes 442376 | tf_op jit(solution)/shard_map/ppermute | solution.py:21
  164.7 37.0 %collective-permute-start.25 = (bf16[72,1024]{1,0:T(8,128)(2,1)}, bf16[72,1024]{1,0:T(8,128)(2,1)}, u32[]{:S(2)}, u32[]{:S(2)}) collective-permute-start(bf16[72,1024]{1,0:T(8,128)(2,1)} %constant_dynamic-update-slice_fusion.16), channel_id=1, source_target_pairs={{0,3},{1,2},{2,1},{3,0},{4,7},{5,6},{6,5},{7,4},{8,11},{9,10},{10,... | collective-permute-start | bytes 442376 | tf_op jit(solution)/shard_map/ppermute | solution.py:21
  217.6 51.3 %collective-permute-start.65 = (bf16[1024,512]{1,0:T(8,128)(2,1)}, bf16[1024,512]{1,0:T(8,128)(2,1)}, u32[]{:S(2)}, u32[]{:S(2)}) collective-permute-start(bf16[1024,512]{1,0:T(8,128)(2,1)} %convolution_convert_fusion), channel_id=1, source_target_pairs={{0,4},{4,0},{8,12},{12,8},{16,20},{20,16},{24,28},{28,24},{1,5},{5... | collective-permute-start | bytes 3145736 | tf_op jit(solution)/shard_map/ppermute | solution.py:21
  240.1 32.6 %collective-permute-start.54 = (bf16[1024,512]{1,0:T(8,128)(2,1)S(1)}, bf16[1024,512]{1,0:T(8,128)(2,1)S(1)}, u32[]{:S(2)}, u32[]{:S(2)}) collective-permute-start(bf16[1024,512]{1,0:T(8,128)(2,1)S(1)} %copy-done.9), channel_id=1, source_target_pairs={{0,4},{4,0},{8,12},{12,8},{16,20},{20,16},{24,28},{28,24},{1,5},{5... | collective-permute-start | bytes 3145736 | tf_op jit(solution)/shard_map/ppermute | solution.py:21
  241.8 32.9 %collective-permute-start.47 = (bf16[512,768]{1,0:T(8,128)(2,1)S(1)}, bf16[512,768]{1,0:T(8,128)(2,1)S(1)}, u32[]{:S(2)}, u32[]{:S(2)}) collective-permute-start(bf16[512,768]{1,0:T(8,128)(2,1)S(1)} %copy-done.49), channel_id=1, source_target_pairs={{0,4},{4,0},{8,12},{12,8},{16,20},{20,16},{24,28},{28,24},{1,5},{5... | collective-permute-start | bytes 2359304 | tf_op jit(solution)/shard_map/ppermute | solution.py:21
  274.7 18.3 %collective-permute-start.67 = (bf16[1024,128]{1,0:T(8,128)(2,1)S(1)}, bf16[1024,128]{1,0:T(8,128)(2,1)S(1)}, u32[]{:S(2)}, u32[]{:S(2)}) collective-permute-start(bf16[1024,128]{1,0:T(8,128)(2,1)S(1)} %get-tuple-element.68), channel_id=1, source_target_pairs={{0,16},{4,20},{8,24},{12,28},{16,0},{20,4},{24,8},{28,12},{1,17},{... | collective-permute-start | bytes 786440 | tf_op jit(solution)/shard_map/ppermute | solution.py:21
  281.7 18.1 %collective-permute-start.57 = (bf16[1024,128]{1,0:T(8,128)(2,1)S(1)}, bf16[1024,128]{1,0:T(8,128)(2,1)S(1)}, u32[]{:S(2)}, u32[]{:S(2)}) collective-permute-start(bf16[1024,128]{1,0:T(8,128)(2,1)S(1)} %get-tuple-element.73), channel_id=1, source_target_pairs={{0,24},{4,28},{8,16},{12,20},{16,8},{20,12},{24,0},{28,4},{1,25},{... | collective-permute-start | bytes 786440 | tf_op jit(solution)/shard_map/ppermute | solution.py:21
  283.5 20.8 %collective-permute-start.56 = (bf16[1024,128]{1,0:T(8,128)(2,1)S(1)}, bf16[1024,128]{1,0:T(8,128)(2,1)S(1)}, u32[]{:S(2)}, u32[]{:S(2)}) collective-permute-start(bf16[1024,128]{1,0:T(8,128)(2,1)S(1)} %get-tuple-element.74), channel_id=1, source_target_pairs={{0,16},{4,20},{8,24},{12,28},{16,0},{20,4},{24,8},{28,12},{1,17},{... | collective-permute-start | bytes 786440 | tf_op jit(solution)/shard_map/ppermute | solution.py:21
  (95 other events, 935.6 us)
where the time goes:
time: 317 us; the launch traced here: 315 us
  waiting for transfers between devices  120 us (38%)
  starting transfers between devices  88.6 us (28%)
  local copies, waits for them, and re-layouts  35.1 us (11%)
  matrix products  28.8 us (9%)
  Pallas kernels  26.4 us (8%)
  other arithmetic  14.8 us (5%)
    ppermute x65, waiting for transfers between devices, swap(): return lax.ppermute(x, axis, [(i, i ^ offset) for i in range(size)])  114 us
    ppermute x65, starting transfers between devices, swap(): return lax.ppermute(x, axis, [(i, i ^ offset) for i in range(size)])  82 us
    unnamed x142, local copies, waits for them, and re-layouts  18.8 us
    dot_general x8, matrix products, tn(): lax.dot_general(a, b, (((0,), (0,)), ((), ())), preferred_element_type=F32)  13.6 us
    pallas_call x5, Pallas kernels, join(): pl.pallas_call(join_kernel, grid=(rows // tile,), in_specs=[pl.BlockSpec(...  13.1 us
    dot_general x6, matrix products, nt(): lax.dot_general(a, b, (((1,), (1,)), ((), ())), preferred_element_type=F32)  7.55 us
    pallas_call x1, Pallas kernels, attend_back(): pl.pallas_call(partial(attend_back_kernel, blocks), out_shape=[jax.ShapeD...  7.33 us
  transfers between devices with their start and end apart: 69, of which 37 were waited for; matrix products, arithmetic and copies ran while one was open for 18% of the time, Pallas kernels for 8%

commit v1 on v0

--- a/solution.py
+++ b/solution.py
@@ -102,7 +102,8 @@
         wanted = place_of(device_index() ^ jnp.arange(size), size)
         parts = lax.all_to_all(jnp.take(pieces, wanted, axis=0), FC, 0, 0, tiled=True)
         return jnp.sum(parts.astype(F32), axis=0)
-    summed = even.astype(F32) + swap(odd.astype(BF), FC, 1).astype(F32)
+    arrived = swap(odd.astype(BF), FC, 1)
+    summed = even.astype(F32) + arrived.astype(F32)
     pieces = jnp.split(summed, half, axis)
     total = pieces[0]
     for o, piece in zip(order(size)[1:half], pieces[1:]):
@@ -283,6 +284,30 @@
     )(q, grad, bias, totals, *kv)
 
 
+def project_kernel(*refs):
+    mixed = jnp.concatenate([ref[...] for ref in refs[:-5]], axis=1)
+    even_ref, odd_ref, resid_ref, shift_ref, out_ref = refs[-5:]
+    half = even_ref.shape[1]
+    for i, weight_ref in enumerate((even_ref, odd_ref)):
+        cols = slice(i * half, (i + 1) * half)
+        out_ref[:, cols] = resid_ref[:, cols] + shift_ref[:, cols] + mm(mixed, weight_ref[...])
+
+
+def project(mixed_pieces, halves, resid, shift):
+    rows, features = resid.shape
+    inner = halves[0].shape[0]
+    return pl.pallas_call(
+        project_kernel,
+        out_shape=jax.ShapeDtypeStruct((rows, features), F32),
+        cost_estimate=pl.CostEstimate(
+            flops=2 * rows * inner * features,
+            bytes_accessed=2 * inner * (rows + features) + 8 * rows * features,
+            transcendentals=0,
+        ),
+        name="project",
+    )(*mixed_pieces, *halves, resid, shift)
+
+
 def local(
     tokens,
     segment_ids,
@@ -355,15 +380,15 @@
     kv = [projected[:, width:]]
     for b in range(1, blocks):
         kv.append(lax.ppermute(kv[0], "ctx", [(i, i + b) for i in range(ctx - b)]))
-    out_full = join(list(gather_columns(out_rows)))
+    out_halves = gather_columns(out_rows)
     ff_halves = gather_columns(ff_shard)
     hidden_width = up_weight.shape[1]
     up_even, up_odd = [w[:hidden_width] for w in ff_halves]
     down_even, down_odd = [w[hidden_width:] for w in ff_halves]
 
     mixed, totals = attend(queries, kv, bias)
-    mixed_all = jnp.concatenate([mixed] + [swap(mixed, "tp", s) for s in range(1, tp)], axis=1)
-    middle = resid + out_shift + jnp.dot(mixed_all, out_full, preferred_element_type=F32)
+    mixed_pieces = [mixed] + [swap(mixed, "tp", s) for s in range(1, tp)]
+    middle = project(mixed_pieces, out_halves, resid, out_shift)
     xhat_two, inverse_two = normalise(middle)
     normed_two = (xhat_two * gain_two + shift_two).astype(BF)
     hidden = nt(normed_two[:, :half], up_even) + nt(normed_two[:, half:], up_odd)
@@ -374,10 +399,10 @@
     grad_active = nt(cot_low[:, :half], down_even) + nt(cot_low[:, half:], down_odd)
     grad_hidden = gelu_pullback(grad_active)[0].astype(BF)
     grad_norm_two = tp_scatter_rows([mm(grad_hidden, up_even), mm(grad_hidden, up_odd)])
-    up_grad = scatter_sum(
-        tn(normed_two[:, :half], grad_hidden), tn(normed_two[:, half:], grad_hidden), 0
-    )
-    down_grad = scatter_sum(tn(active, cot_low[:, :half]), tn(active, cot_low[:, half:]), 1)
+    up_parts = tn(normed_two[:, :half], grad_hidden), tn(normed_two[:, half:], grad_hidden)
+    down_parts = tn(active, cot_low[:, :half]), tn(active, cot_low[:, half:])
+    up_grad = scatter_sum(*up_parts, 0)
+    down_grad = scatter_sum(*down_parts, 1)
     grad_up_bias = jnp.sum(grad_hidden.astype(F32), axis=0)
 
     middle_rows = row_block(middle, t, chunk)
@@ -385,9 +410,10 @@
     cot_rows = row_block(cot_low, t, chunk).astype(F32)
     grad_middle = cot_rows + normalise_back(grad_norm_two, gain_two, xhat_rows, inverse_rows)
     grad_attn = grad_middle.astype(BF)
-    grad_mixed = nt(grad_attn, out_full).astype(BF)
+    grad_mixed = nt(grad_attn[:, :half], out_halves[0]) + nt(grad_attn[:, half:], out_halves[1])
+    grad_mixed = grad_mixed.astype(BF)
     grad_pieces = jnp.split(grad_mixed, tp, axis=1)
-    mixed_rows = row_block(mixed_all, t, chunk)
+    mixed_rows = jnp.concatenate([row_block(m, t, chunk) for m in mixed_pieces], axis=1)
     grad_heads = put_rows([grad_pieces[0]] + [swap(grad_pieces[s], "tp", s) for s in range(1, tp)])
 
     mlp_halves = [mm(active, down_even), mm(active, down_odd)]
@@ -411,9 +437,8 @@
         out_weight_grad = out_weight_grad + swap(out_blocks[s].astype(BF), "tp", s).astype(F32)
 
     grad_norm_one = tp_scatter_rows([mm(grad_joined, in_full)])
-    in_grad = scatter_sum(
-        tn(normed_low[:, :half], grad_joined), tn(normed_low[:, half:], grad_joined), 0
-    )
+    in_parts = tn(normed_low[:, :half], grad_joined), tn(normed_low[:, half:], grad_joined)
+    in_grad = scatter_sum(*in_parts, 0)
     in_weight_grad = jnp.stack([in_grad[:, i * width : (i + 1) * width] for i in range(3)])
     grad_in_bias = jnp.sum(grad_joined.astype(F32), axis=0)
     grad_in_bias = jnp.concatenate([grad_in_bias[:width], grad_in_bias[2 * width :]])

time: 317 us -> 320 us (level)
  local copies, waits for them, and re-layouts: 35.1 us -> 40.8 us
  matrix products: 28.8 us -> 24.5 us
    ppermute x65, waiting for transfers between devices: 114 us -> 108 us  [swap(): return lax.ppermute(x, axis, [(i, i ^ offset) for i in range(size)])]
    unnamed x142 -> x165, local copies, waits for them, and re-layouts: 18.8 us -> 23.4 us
    pallas_call x0 -> x1, Pallas kernels: none -> 3.94 us  [project(): pl.pallas_call(project_kernel, out_shape=jax.ShapeDtypeStruct((rows, feat...]
    pallas_call x5 -> x4, Pallas kernels: 13.1 us -> 10 us  [join(): pl.pallas_call(join_kernel, grid=(rows // tile,), in_specs=[pl.BlockSpec(...]
    dot_general x6 -> x7, matrix products: 7.55 us -> 7.69 us  [nt(): lax.dot_general(a, b, (((1,), (1,)), ((), ())), preferred_element_type=F32)]
  transfers between devices with their start and end apart: 69 -> 69, of which waited for: 37 -> 35; matrix products, arithmetic and copies ran while one was open for 18% -> 19% of each run, Pallas kernels for 8% -> 9%
where the time goes in v1:
time: 320 us; the launch traced here: 318 us
  waiting for transfers between devices  117 us (37%)
  starting transfers between devices  90.2 us (28%)
  local copies, waits for them, and re-layouts  40.8 us (13%)
  Pallas kernels  27.2 us (8%)
  matrix products  24.5 us (8%)
  other arithmetic  17.3 us (5%)
    ppermute x65, waiting for transfers between devices, swap(): return lax.ppermute(x, axis, [(i, i ^ offset) for i in range(size)])  108 us
    ppermute x65, starting transfers between devices, swap(): return lax.ppermute(x, axis, [(i, i ^ offset) for i in range(size)])  83.5 us
    unnamed x165, local copies, waits for them, and re-layouts  23.4 us
    dot_general x8, matrix products, tn(): lax.dot_general(a, b, (((0,), (0,)), ((), ())), preferred_element_type=F32)  11.8 us
    pallas_call x4, Pallas kernels, join(): pl.pallas_call(join_kernel, grid=(rows // tile,), in_specs=[pl.BlockSpec(...  10 us
    dot_general x7, matrix products, nt(): lax.dot_general(a, b, (((1,), (1,)), ((), ())), preferred_element_type=F32)  7.69 us
    pallas_call x1, Pallas kernels, attend_back(): pl.pallas_call(partial(attend_back_kernel, blocks), out_shape=[jax.ShapeD...  7.32 us
  transfers between devices with their start and end apart: 69, of which 35 were waited for; matrix products, arithmetic and copies ran while one was open for 19% of the time, Pallas kernels for 9%

profile of v1, /device:TPU:0, one launch (start us, length us, event | category | flops | bytes accessed | tf_op | source)
XLA Modules:
  0.0 318.3 jit_solution(5444906838142365199)
XLA Ops:
  2.6 3.1 collective-permute-start
  22.2 3.4 %collective-permute-done.11 = bf16[256,128]{1,0:T(8,128)(2,1)S(1)} collective-permute-done((bf16[256,128]{1,0:T(8,128)(2,1)S(1)}, bf16[256,128]{1,0:T(8,128)(2,1)S(1)}, u32[]{:S(2)}, u32[]{:S(2)}) %collective-permute-start.11) | collective-permute-done | bytes 65568 | tf_op jit(solution)/shard_map/ppermute | solution.py:21
  32.1 8.2 %collective-permute-done.12.refs_1_ = bf16[1024,128]{1,0:T(8,128)(2,1)S(1)} collective-permute-done((bf16[1024,128]{1,0:T(8,128)(2,1)S(1)}, bf16[1024,128]{1,0:T(8,128)(2,1)S(1)}, u32[]{:S(2)}, u32[]{:S(2)}) %collective-permute-start.12) | collective-permute-done | bytes 262176 | tf_op jit(solution)/shard_map/ppermute | solution.py:21
  42.1 14.6 %collective-permute-done.13.refs_2_ = bf16[1024,128]{1,0:T(8,128)(2,1)S(1)} collective-permute-done((bf16[1024,128]{1,0:T(8,128)(2,1)S(1)}, bf16[1024,128]{1,0:T(8,128)(2,1)S(1)}, u32[]{:S(2)}, u32[]{:S(2)}) %collective-permute-start.13) | collective-permute-done | bytes 262176 | tf_op jit(solution)/shard_map/ppermute | solution.py:21
  57.2 6.9 %collective-permute-done.14.refs_3_ = bf16[1024,128]{1,0:T(8,128)(2,1)} collective-permute-done((bf16[1024,128]{1,0:T(8,128)(2,1)S(1)}, bf16[1024,128]{1,0:T(8,128)(2,1)}, u32[]{:S(2)}, u32[]{:S(2)}) %collective-permute-start.14) | collective-permute-done | bytes 262176 | tf_op jit(solution)/shard_map/ppermute | solution.py:21
  84.3 5.1 %collective-permute-done.5.refs_4_.refs_7_.refs_6_ = bf16[288,512]{1,0:T(8,128)(2,1)S(1)} collective-permute-done((bf16[288,512]{1,0:T(8,128)(2,1)S(1)}, bf16[288,512]{1,0:T(8,128)(2,1)S(1)}, u32[]{:S(2)}, u32[]{:S(2)}) %collective-permute-start.5) | collective-permute-done | bytes 294944 | tf_op jit(solution)/shard_map/ppermute | solution.py:382
  90.2 5.9 %attend.1 = (bf16[288,256]{1,0:T(8,128)(2,1)}, f32[2,2,288]{2,1,0:T(2,128)}) custom-call(bf16[288,256]{1,0:T(8,128)(2,1)} %slice_multiply_fusion.refs_0_, f32[864,288]{1,0:T(8,128)} %pad_maximum_fusion.refs_1_.refs_2_, bf16[288,512]{1,0:T(8,128)(2,1)} %copy-done.2, bf16[288,512]{1,0:T(8,128)(2,1)} %copy-done.5, bf16[288,512]{1,0:T(8,128)(2,1)} %copy-done.6, ...), custom_call_target="tpu_custom_call" | custom-call | flops 254803968 | bytes 1880064 | tf_op jit(solution)/shard_map/attend/pallas_call | solution.py:252
  96.2 4.1 %collective-permute-start.7 = (bf16[288,256]{1,0:T(8,128)(2,1)}, bf16[288,256]{1,0:T(8,128)(2,1)S(1)}, u32[]{:S(2)}, u32[]{:S(2)}) collective-permute-start(bf16[288,256]{1,0:T(8,128)(2,1)} %get-tuple-element.20.refs_0_), channel_id=1, source_target_pairs={{0,2},{1,3},{2,0},{3,1},{4,6},{5,7},{6,4},{7,5},{8,10},{9,11},{10,... | collective-permute-start | bytes 442376 | tf_op jit(solution)/shard_map/ppermute | solution.py:21
  105.8 5.9 %collective-permute-done.7.refs_2_ = bf16[288,256]{1,0:T(8,128)(2,1)S(1)} collective-permute-done((bf16[288,256]{1,0:T(8,128)(2,1)}, bf16[288,256]{1,0:T(8,128)(2,1)S(1)}, u32[]{:S(2)}, u32[]{:S(2)}) %collective-permute-start.7) | collective-permute-done | bytes 147488 | tf_op jit(solution)/shard_map/ppermute | solution.py:21
  112.4 3.9 %project.1 = f32[288,1024]{1,0:T(8,128)} custom-call(bf16[288,256]{1,0:T(8,128)(2,1)} %get-tuple-element.20.refs_0_, bf16[288,256]{1,0:T(8,128)(2,1)} %copy-done.40, bf16[288,256]{1,0:T(8,128)(2,1)} %copy-done.41, bf16[288,256]{1,0:T(8,128)(2,1)} %copy-done.42, bf16[1024,512]{1,0:T(8,128)(2,1)} %join.6.refs_4_, bf16[1024,512]{1,0:T(8,128)(2,1)} %copy-done.3, ...), custom_call_target="tpu_custom_call" | custom-call | flops 603979776 | bytes 5046272 | tf_op jit(solution)/shard_map/project/pallas_call | solution.py:299
  145.0 6.6 %collective-permute-start.26 = (bf16[72,1024]{1,0:T(8,128)(2,1)S(1)}, bf16[72,1024]{1,0:T(8,128)(2,1)S(1)}, u32[]{:S(2)}, u32[]{:S(2)}) collective-permute-start(bf16[72,1024]{1,0:T(8,128)(2,1)S(1)} %pad_maximum_fusion.9), channel_id=1, source_target_pairs={{0,1},{1,0},{2,3},{3,2},{4,5},{5,4},{6,7},{7,6},{8,9},{9,8},{10,11... | collective-permute-start | bytes 442376 | tf_op jit(solution)/shard_map/ppermute | solution.py:21
  151.6 7.8 %collective-permute-done.21 = bf16[72,1024]{1,0:T(8,128)(2,1)S(1)} collective-permute-done((bf16[72,1024]{1,0:T(8,128)(2,1)S(1)}, bf16[72,1024]{1,0:T(8,128)(2,1)S(1)}, u32[]{:S(2)}, u32[]{:S(2)}) %collective-permute-start.21) | collective-permute-done | bytes 147488 | tf_op jit(solution)/shard_map/ppermute | solution.py:21
  174.8 4.1 %collective-permute-done.29 = bf16[72,256]{1,0:T(8,128)(2,1)S(1)} collective-permute-done((bf16[72,256]{1,0:T(8,128)(2,1)S(1)}, bf16[72,256]{1,0:T(8,128)(2,1)S(1)}, u32[]{:S(2)}, u32[]{:S(2)}) %collective-permute-start.29) | collective-permute-done | bytes 36896 | tf_op jit(solution)/shard_map/ppermute | solution.py:21
  179.5 4.3 %collective-permute-done.30 = bf16[72,256]{1,0:T(8,128)(2,1)S(1)} collective-permute-done((bf16[72,256]{1,0:T(8,128)(2,1)S(1)}, bf16[72,256]{1,0:T(8,128)(2,1)S(1)}, u32[]{:S(2)}, u32[]{:S(2)}) %collective-permute-start.30) | collective-permute-done | bytes 36896 | tf_op jit(solution)/shard_map/ppermute | solution.py:21
  186.2 3.3 %collective-permute-done.31 = bf16[72,256]{1,0:T(8,128)(2,1)S(1)} collective-permute-done((bf16[72,256]{1,0:T(8,128)(2,1)S(1)}, bf16[72,256]{1,0:T(8,128)(2,1)S(1)}, u32[]{:S(2)}, u32[]{:S(2)}) %collective-permute-start.31) | collective-permute-done | bytes 36896 | tf_op jit(solution)/shard_map/ppermute | solution.py:21
  190.2 7.3 %attend_back.1 = (bf16[288,256]{1,0:T(8,128)(2,1)}, f32[288,512]{1,0:T(8,128)}, bf16[288,512]{1,0:T(8,128)(2,1)}, bf16[288,512]{1,0:T(8,128)(2,1)}) custom-call(bf16[288,256]{1,0:T(8,128)(2,1)} %slice_multiply_fusion.refs_0_, bf16[288,256]{1,0:T(8,128)(2,1)} %copy-done.20, f32[864,288]{1,0:T(8,128)} %pad_maximum_fusion.refs_1_.refs_2_, ...), custom_call_target="tpu_custom_call" | custom-call | flops 637009920 | bytes 1880064 | tf_op jit(solution)/shard_map/attend_back/pallas_call | solution.py:274
  203.3 3.2 %collective-permute-done.33 = bf16[288,512]{1,0:T(8,128)(2,1)S(1)} collective-permute-done((bf16[288,512]{1,0:T(8,128)(2,1)}, bf16[288,512]{1,0:T(8,128)(2,1)S(1)}, u32[]{:S(2)}, u32[]{:S(2)}) %collective-permute-start.33) | collective-permute-done | bytes 294944 | tf_op jit(solution)/shard_map/ppermute | solution.py:428
  221.6 4.9 %collective-permute-done.35 = bf16[72,1024]{1,0:T(8,128)(2,1)} collective-permute-done((bf16[72,1024]{1,0:T(8,128)(2,1)}, bf16[72,1024]{1,0:T(8,128)(2,1)}, u32[]{:S(2)}, u32[]{:S(2)}) %collective-permute-start.35) | collective-permute-done | bytes 147488 | tf_op jit(solution)/shard_map/ppermute | solution.py:21
  247.7 3.8 %collective-permute-done.37 = bf16[72,1024]{1,0:T(8,128)(2,1)S(1)} collective-permute-done((bf16[72,1024]{1,0:T(8,128)(2,1)}, bf16[72,1024]{1,0:T(8,128)(2,1)S(1)}, u32[]{:S(2)}, u32[]{:S(2)}) %collective-permute-start.37) | collective-permute-done | bytes 147488 | tf_op jit(solution)/shard_map/ppermute | solution.py:21
  252.9 7.7 %collective-permute-done.38 = bf16[72,1024]{1,0:T(8,128)(2,1)S(1)} collective-permute-done((bf16[72,1024]{1,0:T(8,128)(2,1)}, bf16[72,1024]{1,0:T(8,128)(2,1)S(1)}, u32[]{:S(2)}, u32[]{:S(2)}) %collective-permute-start.38) | collective-permute-done | bytes 147488 | tf_op jit(solution)/shard_map/ppermute | solution.py:21
  263.0 4.8 %collective-permute-done.39 = bf16[72,1024]{1,0:T(8,128)(2,1)S(1)} collective-permute-done((bf16[72,1024]{1,0:T(8,128)(2,1)}, bf16[72,1024]{1,0:T(8,128)(2,1)S(1)}, u32[]{:S(2)}, u32[]{:S(2)}) %collective-permute-start.39) | collective-permute-done | bytes 147488 | tf_op jit(solution)/shard_map/ppermute | solution.py:21
  281.2 4.2 %collective-permute-done.63 = bf16[128,1024]{1,0:T(8,128)(2,1)S(1)} collective-permute-done((bf16[128,1024]{1,0:T(8,128)(2,1)S(1)}, bf16[128,1024]{1,0:T(8,128)(2,1)S(1)}, u32[]{:S(2)}, u32[]{:S(2)}) %collective-permute-start.63) | collective-permute-done | bytes 262176 | tf_op jit(solution)/shard_map/ppermute | solution.py:21
  292.4 4.2 %collective-permute-done.67 = bf16[1024,128]{1,0:T(8,128)(2,1)S(1)} collective-permute-done((bf16[1024,128]{1,0:T(8,128)(2,1)S(1)}, bf16[1024,128]{1,0:T(8,128)(2,1)S(1)}, u32[]{:S(2)}, u32[]{:S(2)}) %collective-permute-start.67) | collective-permute-done | bytes 262176 | tf_op jit(solution)/shard_map/ppermute | solution.py:21
  303.7 4.2 %collective-permute-done.56 = bf16[1024,128]{1,0:T(8,128)(2,1)S(1)} collective-permute-done((bf16[1024,128]{1,0:T(8,128)(2,1)S(1)}, bf16[1024,128]{1,0:T(8,128)(2,1)S(1)}, u32[]{:S(2)}, u32[]{:S(2)}) %collective-permute-start.56) | collective-permute-done | bytes 262176 | tf_op jit(solution)/shard_map/ppermute | solution.py:21
  (414 shorter events, 185.0 us)
Async XLA Ops:
  2.6 25.3 %collective-permute-start = (bf16[800,128]{1,0:T(8,128)(2,1)S(1)}, bf16[800,128]{1,0:T(8,128)(2,1)S(1)}, u32[]{:S(2)}, u32[]{:S(2)}) collective-permute-start(bf16[800,128]{1,0:T(8,128)(2,1)S(1)} %fusion.60.refs_0_), channel_id=1, source_target_pairs={{0,8},{4,12},{8,0},{12,4},{16,24},{20,28},{24,16},{28,20},{1,9},{5... | collective-permute-start | bytes 614408 | tf_op jit(solution)/shard_map/ppermute | solution.py:21
  5.7 23.7 %collective-permute-start.1 = (bf16[800,128]{1,0:T(8,128)(2,1)S(1)}, bf16[800,128]{1,0:T(8,128)(2,1)}, u32[]{:S(2)}, u32[]{:S(2)}) collective-permute-start(bf16[800,128]{1,0:T(8,128)(2,1)S(1)} %fusion.60.refs_0_), channel_id=1, source_target_pairs={{0,16},{4,20},{8,24},{12,28},{16,0},{20,4},{24,8},{28,12},{1,17},{... | collective-permute-start | bytes 614408 | tf_op jit(solution)/shard_map/ppermute | solution.py:21
  7.2 22.7 %collective-permute-start.2 = (bf16[800,128]{1,0:T(8,128)(2,1)S(1)}, bf16[800,128]{1,0:T(8,128)(2,1)}, u32[]{:S(2)}, u32[]{:S(2)}) collective-permute-start(bf16[800,128]{1,0:T(8,128)(2,1)S(1)} %fusion.60.refs_0_), channel_id=1, source_target_pairs={{0,24},{4,28},{8,16},{12,20},{16,8},{20,12},{24,0},{28,4},{1,25},{... | collective-permute-start | bytes 614408 | tf_op jit(solution)/shard_map/ppermute | solution.py:21
  19.6 46.9 %collective-permute-start.16 = (bf16[2048,128]{1,0:T(8,128)(2,1)S(1)}, bf16[2048,128]{1,0:T(8,128)(2,1)S(1)}, u32[]{:S(2)}, u32[]{:S(2)}) collective-permute-start(bf16[2048,128]{1,0:T(8,128)(2,1)S(1)} %pad_maximum_fusion.1.refs_0_), channel_id=1, source_target_pairs={{0,8},{4,12},{8,0},{12,4},{16,24},{20,28},{24,16},{28,20},{1,9},{5... | collective-permute-start | bytes 1572872 | tf_op jit(solution)/shard_map/ppermute | solution.py:21
  27.9 38.6 %collective-permute-start.17 = (bf16[2048,128]{1,0:T(8,128)(2,1)S(1)}, bf16[2048,128]{1,0:T(8,128)(2,1)}, u32[]{:S(2)}, u32[]{:S(2)}) collective-permute-start(bf16[2048,128]{1,0:T(8,128)(2,1)S(1)} %pad_maximum_fusion.1.refs_0_), channel_id=1, source_target_pairs={{0,16},{4,20},{8,24},{12,28},{16,0},{20,4},{24,8},{28,12},{1,17},{... | collective-permute-start | bytes 1572872 | tf_op jit(solution)/shard_map/ppermute | solution.py:21
  29.4 37.1 %collective-permute-start.18 = (bf16[2048,128]{1,0:T(8,128)(2,1)S(1)}, bf16[2048,128]{1,0:T(8,128)(2,1)}, u32[]{:S(2)}, u32[]{:S(2)}) collective-permute-start(bf16[2048,128]{1,0:T(8,128)(2,1)S(1)} %pad_maximum_fusion.1.refs_0_), channel_id=1, source_target_pairs={{0,24},{4,28},{8,16},{12,20},{16,8},{20,12},{24,0},{28,4},{1,25},{... | collective-permute-start | bytes 1572872 | tf_op jit(solution)/shard_map/ppermute | solution.py:21
  32.1 38.4 %collective-permute-start.3 = (bf16[800,512]{1,0:T(8,128)(2,1)}, bf16[800,512]{1,0:T(8,128)(2,1)S(1)}, u32[]{:S(2)}, u32[]{:S(2)}) collective-permute-start(bf16[800,512]{1,0:T(8,128)(2,1)} %join.4.refs_0_), channel_id=1, source_target_pairs={{0,4},{4,0},{8,12},{12,8},{16,20},{20,16},{24,28},{28,24},{1,5},{5... | collective-permute-start | bytes 2457608 | tf_op jit(solution)/shard_map/ppermute | solution.py:21
  66.5 38.2 %collective-permute-start.15 = (bf16[1024,512]{1,0:T(8,128)(2,1)}, bf16[1024,512]{1,0:T(8,128)(2,1)S(1)}, u32[]{:S(2)}, u32[]{:S(2)}) collective-permute-start(bf16[1024,512]{1,0:T(8,128)(2,1)} %join.6.refs_4_), channel_id=1, source_target_pairs={{0,4},{4,0},{8,12},{12,8},{16,20},{20,16},{24,28},{28,24},{1,5},{5... | collective-permute-start | bytes 3145736 | tf_op jit(solution)/shard_map/ppermute | solution.py:21
  70.0 50.9 %collective-permute-start.19 = (bf16[2048,512]{1,0:T(8,128)(2,1)}, bf16[2048,512]{1,0:T(8,128)(2,1)}, u32[]{:S(2)}, u32[]{:S(2)}) collective-permute-start(bf16[2048,512]{1,0:T(8,128)(2,1)} %join.7), channel_id=1, source_target_pairs={{0,4},{4,0},{8,12},{12,8},{16,20},{20,16},{24,28},{28,24},{1,5},{5... | collective-permute-start | bytes 6291464 | tf_op jit(solution)/shard_map/ppermute | solution.py:21
  138.7 20.7 %collective-permute-start.21 = (bf16[72,1024]{1,0:T(8,128)(2,1)S(1)}, bf16[72,1024]{1,0:T(8,128)(2,1)S(1)}, u32[]{:S(2)}, u32[]{:S(2)}) collective-permute-start(bf16[72,1024]{1,0:T(8,128)(2,1)S(1)} %pad_maximum_fusion.7), channel_id=1, source_target_pairs={{0,2},{1,3},{2,0},{3,1},{4,6},{5,7},{6,4},{7,5},{8,10},{9,11},{10,... | collective-permute-start | bytes 442376 | tf_op jit(solution)/shard_map/ppermute | solution.py:21
  141.2 18.2 %collective-permute-start.20 = (bf16[72,1024]{1,0:T(8,128)(2,1)S(1)}, bf16[72,1024]{1,0:T(8,128)(2,1)S(1)}, u32[]{:S(2)}, u32[]{:S(2)}) collective-permute-start(bf16[72,1024]{1,0:T(8,128)(2,1)S(1)} %pad_maximum_fusion.6), channel_id=1, source_target_pairs={{0,1},{1,0},{2,3},{3,2},{4,5},{5,4},{6,7},{7,6},{8,9},{9,8},{10,11... | collective-permute-start | bytes 442376 | tf_op jit(solution)/shard_map/ppermute | solution.py:21
  141.4 23.0 %collective-permute-start.28 = (bf16[72,1024]{1,0:T(8,128)(2,1)S(1)}, bf16[72,1024]{1,0:T(8,128)(2,1)S(1)}, u32[]{:S(2)}, u32[]{:S(2)}) collective-permute-start(bf16[72,1024]{1,0:T(8,128)(2,1)S(1)} %pad_maximum_fusion.11), channel_id=1, source_target_pairs={{0,3},{1,2},{2,1},{3,0},{4,7},{5,6},{6,5},{7,4},{8,11},{9,10},{10,... | collective-permute-start | bytes 442376 | tf_op jit(solution)/shard_map/ppermute | solution.py:21
  143.8 23.6 %collective-permute-start.27 = (bf16[72,1024]{1,0:T(8,128)(2,1)S(1)}, bf16[72,1024]{1,0:T(8,128)(2,1)S(1)}, u32[]{:S(2)}, u32[]{:S(2)}) collective-permute-start(bf16[72,1024]{1,0:T(8,128)(2,1)S(1)} %pad_maximum_fusion.10), channel_id=1, source_target_pairs={{0,2},{1,3},{2,0},{3,1},{4,6},{5,7},{6,4},{7,5},{8,10},{9,11},{10,... | collective-permute-start | bytes 442376 | tf_op jit(solution)/shard_map/ppermute | solution.py:21
  145.0 23.8 %collective-permute-start.26 = (bf16[72,1024]{1,0:T(8,128)(2,1)S(1)}, bf16[72,1024]{1,0:T(8,128)(2,1)S(1)}, u32[]{:S(2)}, u32[]{:S(2)}) collective-permute-start(bf16[72,1024]{1,0:T(8,128)(2,1)S(1)} %pad_maximum_fusion.9), channel_id=1, source_target_pairs={{0,1},{1,0},{2,3},{3,2},{4,5},{5,4},{6,7},{7,6},{8,9},{9,8},{10,11... | collective-permute-start | bytes 442376 | tf_op jit(solution)/shard_map/ppermute | solution.py:21
  159.4 108.4 %collective-permute-start.61 = (bf16[512,1024]{1,0:T(8,128)(2,1)}, bf16[512,1024]{1,0:T(8,128)(2,1)}, u32[]{:S(2)}, u32[]{:S(2)}) collective-permute-start(bf16[512,1024]{1,0:T(8,128)(2,1)} %convolution_convert_fusion.1), channel_id=1, source_target_pairs={{0,4},{4,0},{8,12},{12,8},{16,20},{20,16},{24,28},{28,24},{1,5},{5... | collective-permute-start | bytes 3145736 | tf_op jit(solution)/shard_map/ppermute | solution.py:21
  164.4 34.5 %collective-permute-start.23 = (bf16[72,1024]{1,0:T(8,128)(2,1)}, bf16[72,1024]{1,0:T(8,128)(2,1)}, u32[]{:S(2)}, u32[]{:S(2)}) collective-permute-start(bf16[72,1024]{1,0:T(8,128)(2,1)} %constant_dynamic-update-slice_fusion.12), channel_id=1, source_target_pairs={{0,1},{1,0},{2,3},{3,2},{4,5},{5,4},{6,7},{7,6},{8,9},{9,8},{10,11... | collective-permute-start | bytes 442376 | tf_op jit(solution)/shard_map/ppermute | solution.py:21
  164.4 36.9 %collective-permute-start.24 = (bf16[72,1024]{1,0:T(8,128)(2,1)}, bf16[72,1024]{1,0:T(8,128)(2,1)}, u32[]{:S(2)}, u32[]{:S(2)}) collective-permute-start(bf16[72,1024]{1,0:T(8,128)(2,1)} %constant_dynamic-update-slice_fusion.12), channel_id=1, source_target_pairs={{0,2},{1,3},{2,0},{3,1},{4,6},{5,7},{6,4},{7,5},{8,10},{9,11},{10,... | collective-permute-start | bytes 442376 | tf_op jit(solution)/shard_map/ppermute | solution.py:21
  167.4 34.9 %collective-permute-start.25 = (bf16[72,1024]{1,0:T(8,128)(2,1)}, bf16[72,1024]{1,0:T(8,128)(2,1)}, u32[]{:S(2)}, u32[]{:S(2)}) collective-permute-start(bf16[72,1024]{1,0:T(8,128)(2,1)} %constant_dynamic-update-slice_fusion.12), channel_id=1, source_target_pairs={{0,3},{1,2},{2,1},{3,0},{4,7},{5,6},{6,5},{7,4},{8,11},{9,10},{10,... | collective-permute-start | bytes 442376 | tf_op jit(solution)/shard_map/ppermute | solution.py:21
  220.4 52.2 %collective-permute-start.65 = (bf16[1024,512]{1,0:T(8,128)(2,1)}, bf16[1024,512]{1,0:T(8,128)(2,1)}, u32[]{:S(2)}, u32[]{:S(2)}) collective-permute-start(bf16[1024,512]{1,0:T(8,128)(2,1)} %convolution_convert_fusion), channel_id=1, source_target_pairs={{0,4},{4,0},{8,12},{12,8},{16,20},{20,16},{24,28},{28,24},{1,5},{5... | collective-permute-start | bytes 3145736 | tf_op jit(solution)/shard_map/ppermute | solution.py:21
  243.7 32.4 %collective-permute-start.54 = (bf16[1024,512]{1,0:T(8,128)(2,1)S(1)}, bf16[1024,512]{1,0:T(8,128)(2,1)S(1)}, u32[]{:S(2)}, u32[]{:S(2)}) collective-permute-start(bf16[1024,512]{1,0:T(8,128)(2,1)S(1)} %copy-done.13), channel_id=1, source_target_pairs={{0,4},{4,0},{8,12},{12,8},{16,20},{20,16},{24,28},{28,24},{1,5},{5... | collective-permute-start | bytes 3145736 | tf_op jit(solution)/shard_map/ppermute | solution.py:21
  245.0 32.5 %collective-permute-start.47 = (bf16[512,768]{1,0:T(8,128)(2,1)S(1)}, bf16[512,768]{1,0:T(8,128)(2,1)S(1)}, u32[]{:S(2)}, u32[]{:S(2)}) collective-permute-start(bf16[512,768]{1,0:T(8,128)(2,1)S(1)} %copy-done.62), channel_id=1, source_target_pairs={{0,4},{4,0},{8,12},{12,8},{16,20},{20,16},{24,28},{28,24},{1,5},{5... | collective-permute-start | bytes 2359304 | tf_op jit(solution)/shard_map/ppermute | solution.py:21
  277.5 19.1 %collective-permute-start.67 = (bf16[1024,128]{1,0:T(8,128)(2,1)S(1)}, bf16[1024,128]{1,0:T(8,128)(2,1)S(1)}, u32[]{:S(2)}, u32[]{:S(2)}) collective-permute-start(bf16[1024,128]{1,0:T(8,128)(2,1)S(1)} %get-tuple-element.68), channel_id=1, source_target_pairs={{0,16},{4,20},{8,24},{12,28},{16,0},{20,4},{24,8},{28,12},{1,17},{... | collective-permute-start | bytes 786440 | tf_op jit(solution)/shard_map/ppermute | solution.py:21
  280.5 18.3 %collective-permute-start.66 = (bf16[1024,128]{1,0:T(8,128)(2,1)S(1)}, bf16[1024,128]{1,0:T(8,128)(2,1)S(1)}, u32[]{:S(2)}, u32[]{:S(2)}) collective-permute-start(bf16[1024,128]{1,0:T(8,128)(2,1)S(1)} %get-tuple-element.66), channel_id=1, source_target_pairs={{0,8},{4,12},{8,0},{12,4},{16,24},{20,28},{24,16},{28,20},{1,9},{5... | collective-permute-start | bytes 786440 | tf_op jit(solution)/shard_map/ppermute | solution.py:21
  287.5 20.3 %collective-permute-start.56 = (bf16[1024,128]{1,0:T(8,128)(2,1)S(1)}, bf16[1024,128]{1,0:T(8,128)(2,1)S(1)}, u32[]{:S(2)}, u32[]{:S(2)}) collective-permute-start(bf16[1024,128]{1,0:T(8,128)(2,1)S(1)} %get-tuple-element.74), channel_id=1, source_target_pairs={{0,16},{4,20},{8,24},{12,28},{16,0},{20,4},{24,8},{28,12},{1,17},{... | collective-permute-start | bytes 786440 | tf_op jit(solution)/shard_map/ppermute | solution.py:21
  (108 other events, 792.4 us)
